TPU v7x, 32 devices: a whole 2x2x4 slice. The times are simulated.
32 devices in a mesh: scene: 8 (over z, x), tie: 4 (over y, core).
Axes of the slice: x: 2, y: 2, z: 4, core: 2. Of those that a mesh axis runs over, the one named last changes fastest.
Arguments:
- tie_rows: bfloat16 [384, 256, 256], P('tie'), may hold values from -0.375 to 0.375
- point_counts: int32 [384], P('tie'), may hold values from 1 to 128, as said below
- pattern: int32 [128, 384], P('scene', 'tie'), may hold values 0 or 1
- sensitivity: bfloat16 [128, 192, 192], P('scene'), may hold values from -0.119628906 to 0.119628906
- damping: float32 [128], P(('scene', 'tie')), may hold values from 1 to 8
- prior: float32 [64], replicated, may hold values from 0.25 to 4
Outputs:
- scene_rows: float32 [128, 192, 256], P(('scene', 'tie'))
- global_factor: float32 [64, 64], replicated
Inputs may be any that keep to these rules, and one draw needn't show every extreme that they name: `point_counts`: points present in each block; some block is full.
All inputs are finite; a program needn't handle non-finite values. No bound on the sum of `pattern` on one device may be relied on, other than what follows from the above.
Results may differ from a plain program's by a relative error of at most 0.0003.
Values sent between devices are 32-bit elements; how exact they have to be, the bound alone decides.
A program may use at most 128 MiB of HBM per device.

v0:
```python
import functools
import math

import jax
import jax.numpy as jnp
from jax import lax
from jax.experimental import pallas as pl
from jax.experimental.pallas import tpu as pltpu
from jax.sharding import PartitionSpec as P

MESH = pl.DeviceIdType.MESH
HIGHEST = lax.Precision.HIGHEST
F32 = jnp.float32
BF16 = jnp.bfloat16
PANEL = 32
LANES = 128
VMEM = pl.BlockSpec(memory_space=pltpu.VMEM)


def over_rows(a, b, precision=None):
    return lax.dot_general(
        a, b, (((0,), (0,)), ((), ())), precision=precision, preferred_element_type=F32
    )


def gram_kernel(chunk, most, counts, order, active, rows_ref, out_ref, gram_ref):
    step = pl.program_id(0)

    @pl.when(step == 0)
    def _():
        out_ref[...] = jnp.zeros_like(out_ref)

    half = rows_ref.shape[2] // 2
    row_index = lax.broadcasted_iota(jnp.int32, rows_ref.shape[1:], 0)
    for i in range(chunk):
        rows = rows_ref[i]
        valid = jnp.where(row_index < 2 * counts[step * chunk + i], 1.0, 0.0).astype(BF16)
        kept = rows * valid
        top = over_rows(kept[:, :half], rows)
        gram_ref[i, :half] = top[:, :half]
        gram_ref[i, half : 2 * half] = top[:, half:]
        gram_ref[i, 2 * half :] = over_rows(kept[:, half:], rows[:, half:])
    for i in range(chunk):
        block = step * chunk + i

        def add(k, carry, i=i, block=block):
            scene = order[block * most + k]
            out_ref[scene] += gram_ref[i]
            return carry

        lax.fori_loop(0, active[block], add, 0)


def merged_partials(tie_rows, point_counts, pattern):
    blocks, rows, width = tie_rows.shape
    scenes = pattern.shape[0]
    half = width // 2
    chunk = math.gcd(blocks, 8)
    index = jnp.arange(scenes)
    seen = (pattern != 0).astype(jnp.int32).T
    before = jnp.sum(seen[:, None, :] * (index[None, :] < index[:, None])[None], 2)
    hits = (before[:, :, None] == index) & (seen[:, :, None] != 0)
    order = jnp.sum(jnp.where(hits, index[None, :, None], 0), 1).reshape(-1)
    return pl.pallas_call(
        functools.partial(gram_kernel, chunk, scenes),
        grid_spec=pltpu.PrefetchScalarGridSpec(
            num_scalar_prefetch=3,
            grid=(blocks // chunk,),
            in_specs=[pl.BlockSpec((chunk, rows, width), lambda i, *_: (i, 0, 0))],
            out_specs=pl.BlockSpec((scenes, 3 * half, half), lambda i, *_: (0, 0, 0)),
            scratch_shapes=[pltpu.VMEM((chunk, 3 * half, half), F32)],
        ),
        out_shape=jax.ShapeDtypeStruct((scenes, 3 * half, half), F32),
        name="grams",
    )(point_counts, order.astype(jnp.int32), jnp.sum(seen, 1), tie_rows)


def scatter_kernel(n, own, part, out, got, summed, far, s1, r1, s2, r2):
    me = lax.axis_index("tie")
    pairs = n // 2
    parity = lax.rem(me, 2)
    group = me // 2
    partner = me + 1 - 2 * parity

    def member(k, side):
        return lax.rem(group + k, pairs) * 2 + side

    barrier = pltpu.get_barrier_semaphore()
    pl.semaphore_signal(barrier, inc=1, device_id={"tie": partner}, device_id_type=MESH)
    for k in range(1, pairs):
        pl.semaphore_signal(
            barrier, inc=1, device_id={"tie": member(k, parity)}, device_id_type=MESH
        )
    pl.semaphore_wait(barrier, pairs)

    order = [(k, q) for k in list(range(1, pairs)) + [0] for q in range(own)]
    first, second = {}, {}
    for k, q in order:
        slot = k * own + q
        first[k, q] = pltpu.make_async_remote_copy(
            src_ref=part.at[member(k, 1 - parity) * own + q],
            dst_ref=got.at[slot],
            send_sem=s1.at[slot],
            recv_sem=r1.at[slot],
            device_id={"tie": partner},
            device_id_type=MESH,
        )
        first[k, q].start()
    for k, q in order:
        slot = k * own + q
        first[k, q].wait_recv()
        mine = member(k, parity) * own + q
        if k == 0:
            out[q] = part[mine] + got[slot]
        else:
            summed[slot] = part[mine] + got[slot]
            second[k, q] = pltpu.make_async_remote_copy(
                src_ref=summed.at[slot],
                dst_ref=far.at[slot],
                send_sem=s2.at[slot],
                recv_sem=r2.at[slot],
                device_id={"tie": member(k, parity)},
                device_id_type=MESH,
            )
            second[k, q].start()
    for k, q in order:
        if k:
            second[k, q].wait_recv()
            out[q] += far[k * own + q]
    for k, q in order:
        first[k, q].wait_send()
        if k:
            second[k, q].wait_send()


def scatter_sum(partials, n):
    scenes, high, wide = partials.shape
    own = scenes // n
    slots = own * (n // 2)
    block = (slots, high, wide)
    dma = pltpu.SemaphoreType.DMA((slots,))
    return pl.pallas_call(
        functools.partial(scatter_kernel, n, own),
        out_shape=jax.ShapeDtypeStruct((own, high, wide), F32),
        in_specs=[VMEM],
        out_specs=VMEM,
        scratch_shapes=[pltpu.VMEM(block, F32)] * 3 + [dma] * 4,
        compiler_params=pltpu.CompilerParams(collective_id=0, has_side_effects=True),
        name="scatter",
    )(partials)


def three_parts(x):
    high = x.astype(BF16)
    rest = x - high.astype(F32)
    middle = rest.astype(BF16)
    return high, middle, (rest - middle.astype(F32)).astype(BF16)


def eliminate(panels, first_column):
    shape = panels[0].shape
    row_index = lax.broadcasted_iota(jnp.int32, shape, 0)
    lane = lax.broadcasted_iota(jnp.int32, shape, 1)
    for j in range(shape[0]):
        c = first_column + j
        for q, panel in enumerate(panels):
            column = jnp.broadcast_to(panel[:, c : c + 1], shape)
            scaled = panel[j : j + 1] / column[j : j + 1]
            panels[q] = panel - jnp.where(row_index > j, column, 0.0) * scaled
    above = lane >= row_index + first_column
    on_diagonal = lane == row_index + first_column
    done = []
    for panel in panels:
        diagonal = jnp.sum(jnp.where(on_diagonal, panel, 0.0), 1, keepdims=True)
        root = jnp.broadcast_to(jnp.sqrt(diagonal), shape)
        done.append(jnp.where(above, panel / root, 0.0))
    return done


def factor_kernel(damping, merged, sens, out, reduced, info):
    own, width, _ = info.shape
    spline = out.shape[1]
    half = width // 2
    row_index = lax.broadcasted_iota(jnp.int32, (width, width), 0)
    lane = lax.broadcasted_iota(jnp.int32, (width, width), 1)
    on_diagonal = (row_index == lane) & (row_index < spline)
    for q in range(own):
        side = merged[q, half : 2 * half]
        top = jnp.concatenate([merged[q, :half], side], 1)
        bottom = jnp.concatenate([side.T, merged[q, 2 * half :]], 1)
        whole = jnp.concatenate([top, bottom], 0)
        s = sens[q]
        mixed = whole
        for piece in three_parts(whole):
            mixed = mixed + jnp.dot(piece, s, preferred_element_type=F32)
        result = mixed + over_rows(s.astype(F32), mixed, HIGHEST)
        info[q] = result + jnp.where(on_diagonal, damping[q], 0.0)
    for start in range(0, spline, PANEL):
        base = start // LANES * LANES
        panels = [info[q, start : start + PANEL, base:] for q in range(own)]
        rows = eliminate(panels, start - base)
        for q in range(own):
            out[q, start : start + PANEL, base:] = rows[q]
        if base:
            out[:, start : start + PANEL, :base] = jnp.zeros((own, PANEL, base), F32)
        after = start + PANEL
        for q in range(own):
            info[q, after:, base:] -= over_rows(
                rows[q], rows[q], HIGHEST
            )[after - base :]
    total = info[0, spline:, half:]
    for q in range(1, own):
        total = total + info[q, spline:, half:]
    reduced[...] = total


def factor_scenes(merged, sensitivity, damping, width):
    own = damping.shape[0]
    spline = sensitivity.shape[1]
    half = width // 2
    mine = lax.dynamic_slice_in_dim(sensitivity, lax.axis_index("tie") * own, own)
    beyond = width - spline
    mine = jnp.pad(mine, ((0, 0), (0, beyond), (0, beyond)))
    return pl.pallas_call(
        factor_kernel,
        in_specs=[pl.BlockSpec(memory_space=pltpu.SMEM), VMEM, VMEM],
        out_specs=[VMEM, VMEM],
        scratch_shapes=[pltpu.VMEM((own, width, width), F32)],
        out_shape=[
            jax.ShapeDtypeStruct((own, spline, width), F32),
            jax.ShapeDtypeStruct((width - spline, half), F32),
        ],
        name="factor",
    )(damping, merged, mine)


def total_kernel(axes, x, out, *scratch):
    barrier = pltpu.get_barrier_semaphore()
    for name, n in axes:
        me = lax.axis_index(name)
        for k in range(1, n):
            pl.semaphore_signal(
                barrier, inc=1, device_id={name: lax.rem(me + k, n)}, device_id_type=MESH
            )
    pl.semaphore_wait(barrier, sum(n - 1 for _, n in axes))
    value = x
    for at, (name, n) in enumerate(axes):
        slots, send, recv = scratch[3 * at : 3 * at + 3]
        me = lax.axis_index(name)
        slots[0] = value[...]
        copies = []
        for k in range(1, n):
            copies.append(
                pltpu.make_async_remote_copy(
                    src_ref=slots.at[0],
                    dst_ref=slots.at[k],
                    send_sem=send.at[k],
                    recv_sem=recv.at[k],
                    device_id={name: lax.rem(me + k, n)},
                    device_id_type=MESH,
                )
            )
            copies[-1].start()
        for copy in copies:
            copy.wait_recv()
        acc = slots[me]
        for i in range(1, n):
            acc = acc + slots[lax.rem(me - i + n, n)]
        for copy in copies:
            copy.wait_send()
        out[...] = acc
        value = out


def total_sum(x, axes):
    scratch = []
    for _, n in axes:
        scratch += [pltpu.VMEM((n,) + x.shape, F32)]
        scratch += [pltpu.SemaphoreType.DMA((n,))] * 2
    return pl.pallas_call(
        functools.partial(total_kernel, axes),
        out_shape=jax.ShapeDtypeStruct(x.shape, F32),
        in_specs=[VMEM],
        out_specs=VMEM,
        scratch_shapes=scratch,
        compiler_params=pltpu.CompilerParams(collective_id=1, has_side_effects=True),
        name="total",
    )(x)


def last_kernel(scale, x, prior, out):
    shared, wide = x.shape
    lane = lax.broadcasted_iota(jnp.int32, (shared, wide), 1)
    row = lax.broadcasted_iota(jnp.int32, (shared, wide), 0) + wide - shared
    value = x[...] * scale + jnp.where(lane == row, prior[...], 0.0)
    out[...] = eliminate([value], wide - shared)[0][:, wide - shared :]


def last_factor(x, prior, scale):
    shared = x.shape[0]
    return pl.pallas_call(
        functools.partial(last_kernel, scale),
        out_shape=jax.ShapeDtypeStruct((shared, shared), F32),
        in_specs=[VMEM, VMEM],
        out_specs=VMEM,
        name="last",
    )(x, prior[:, None])


def on_device(axes, tie_rows, point_counts, pattern, sensitivity, damping, prior):
    sizes = dict(axes)
    width = tie_rows.shape[2]
    partials = merged_partials(tie_rows, point_counts, pattern)
    merged = scatter_sum(partials, sizes["tie"])
    scene_rows, reduced = factor_scenes(merged, sensitivity, damping, width)
    total = total_sum(reduced, axes)
    scenes = damping.shape[0] * math.prod(sizes.values())
    return scene_rows, last_factor(total, prior, 1.0 / scenes)


def solution(mesh):
    axes = (("tie", mesh.shape["tie"]), ("scene", mesh.shape["scene"]))
    placed = (
        P("tie", None, None),
        P("tie"),
        P("scene", "tie"),
        P("scene", None, None),
        P(("scene", "tie")),
        P(),
    )
    return jax.shard_map(
        functools.partial(on_device, axes),
        mesh=mesh,
        in_specs=placed,
        out_specs=(P(("scene", "tie"), None, None), P()),
        check_vma=False,
    )
```

profile of v0, /device:TPU:0, one launch (start us, length us, event | category | flops | bytes accessed | tf_op | source)
XLA Modules:
  0.0 92.6 jit_solution(17881962040873065255)
XLA Ops:
  0.6 0.0 copy-start
  0.7 1.3 %convert_reduce_fusion = (s32[96]{0:T(128)}, pred[16,96]{1,0:T(8,128)(4,1)S(1)}) fusion(s32[16,96]{1,0:T(8,128)} %param.8), kind=kLoop, calls=%fused_computation.4 | loop fusion | flops 4512 | bytes 8064 | tf_op jit(solution)/shard_map/reduce_sum | solution.py:75
  2.0 0.1 multiply_reduce_fusion
  2.2 0.1 copy.14
  2.3 0.7 reshape.25.order
  3.0 15.6 %grams.1.part = f32[16,384,128]{2,1,0:T(8,128)} custom-call(s32[96]{0:T(128)} %counts.1, s32[1536]{0:T(1024)} %reshape.25.order, s32[96]{0:T(128)} %get-tuple-element.6.active, bf16[96,256,256]{2,1,0:T(8,128)(2,1)} %rows_ref.1), custom_call_target="tpu_custom_call" | custom-call | tf_op jit(solution)/shard_map/grams/pallas_call | solution.py:64
  18.5 0.0 copy-start.1
  18.5 25.5 %scatter.1.merged = f32[4,384,128]{2,1,0:T(8,128)} custom-call(f32[16,384,128]{2,1,0:T(8,128)} %grams.1.part), custom_call_target="tpu_custom_call" | custom-call | tf_op jit(solution)/shard_map/scatter/pallas_call | solution.py:142
  44.1 0.0 copy-done
  44.1 0.9 pad.4.sens
  45.0 25.0 %factor.1 = (f32[4,192,256]{2,1,0:T(8,128)}, f32[64,128]{1,0:T(8,128)}) custom-call(f32[4]{0:T(128)} %damping.1, f32[4,384,128]{2,1,0:T(8,128)} %scatter.1.merged, bf16[4,256,256]{2,1,0:T(8,128)(2,1)} %pad.4.sens), custom_call_target="tpu_custom_call" | custom-call | tf_op jit(solution)/shard_map/factor/pallas_call | solution.py:224
  70.0 14.9 %total.1.x = f32[64,128]{1,0:T(8,128)} custom-call(f32[64,128]{1,0:T(8,128)} %get-tuple-element.5.x), custom_call_target="tpu_custom_call" | custom-call | tf_op jit(solution)/shard_map/total/pallas_call | solution.py:280
  84.9 0.0 copy-done.1
  85.0 0.7 copy.15.prior
  85.6 6.9 %last.1 = f32[64,64]{1,0:T(8,128)} custom-call(f32[64,128]{1,0:T(8,128)} %total.1.x, f32[64,1]{1,0:T(8,128)} %copy.15.prior), custom_call_target="tpu_custom_call" | custom-call | tf_op jit(solution)/shard_map/last/pallas_call | solution.py:301
  (5 shorter events, 0.1 us)
Async XLA Ops:
  0.6 43.4 %copy-start = (bf16[16,192,192]{2,1,0:T(8,128)(2,1)S(1)}, bf16[16,192,192]{2,1,0:T(8,128)(2,1)}, u32[]{:S(2)}) copy-start(bf16[16,192,192]{2,1,0:T(8,128)(2,1)} %param.9) | copy-start | bytes 3538948
  18.5 66.4 %copy-start.1 = (f32[64]{0:T(128)S(1)}, f32[64]{0:T(128)}, u32[]{:S(2)}) copy-start(f32[64]{0:T(128)} %param.11) | copy-start | bytes 772
where the time goes:
time: 92.9 us; the launch traced here: 92.6 us
  Pallas kernels  88 us (95%)
  local copies, waits for them, and re-layouts  2.38 us (3%)
  other arithmetic  1.5 us (2%)
    pallas_call x1, Pallas kernels, scatter_sum(): pl.pallas_call(functools.partial(scatter_kernel, n, own), out_shape=jax.S...  25.5 us
    pallas_call x1, Pallas kernels, factor_scenes(): pl.pallas_call(factor_kernel, in_specs=[pl.BlockSpec(memory_space=pltpu.S...  25 us
    pallas_call x1, Pallas kernels, merged_partials(): pl.pallas_call(functools.partial(gram_kernel, chunk, scenes), grid_spec=p...  15.6 us
    pallas_call x1, Pallas kernels, total_sum(): pl.pallas_call(functools.partial(total_kernel, axes), out_shape=jax.Shape...  14.9 us
    pallas_call x1, Pallas kernels, last_factor(): pl.pallas_call(functools.partial(last_kernel, scale), out_shape=jax.Shape...  6.93 us

commit v1 on v0

--- a/solution.py
+++ b/solution.py
@@ -204,14 +204,16 @@
         if base:
             out[:, start : start + PANEL, :base] = jnp.zeros((own, PANEL, base), F32)
         after = start + PANEL
+        left = after // LANES * LANES
         for q in range(own):
-            info[q, after:, base:] -= over_rows(
-                rows[q], rows[q], HIGHEST
-            )[after - base :]
+            rest = rows[q][:, left - base :]
+            info[q, after:, left:] -= over_rows(rest, rest, HIGHEST)[after - left :]
     total = info[0, spline:, half:]
     for q in range(1, own):
         total = total + info[q, spline:, half:]
-    reduced[...] = total
+    total = total[:, spline - half :]
+    middle = (width - spline) // 2
+    reduced[...] = jnp.concatenate([total[:middle], total[middle:]], 1)
 
 
 def factor_scenes(merged, sensitivity, damping, width):
@@ -228,7 +230,7 @@
         scratch_shapes=[pltpu.VMEM((own, width, width), F32)],
         out_shape=[
             jax.ShapeDtypeStruct((own, spline, width), F32),
-            jax.ShapeDtypeStruct((width - spline, half), F32),
+            jax.ShapeDtypeStruct(((width - spline) // 2, 2 * (width - spline)), F32),
         ],
         name="factor",
     )(damping, merged, mine)
@@ -289,15 +291,17 @@
 
 
 def last_kernel(scale, x, prior, out):
-    shared, wide = x.shape
-    lane = lax.broadcasted_iota(jnp.int32, (shared, wide), 1)
-    row = lax.broadcasted_iota(jnp.int32, (shared, wide), 0) + wide - shared
-    value = x[...] * scale + jnp.where(lane == row, prior[...], 0.0)
-    out[...] = eliminate([value], wide - shared)[0][:, wide - shared :]
+    shared = prior.shape[0]
+    lane = lax.broadcasted_iota(jnp.int32, (shared, shared), 1)
+    row = lax.broadcasted_iota(jnp.int32, (shared, shared), 0)
+    packed = x[...]
+    value = jnp.concatenate([packed[:, :shared], packed[:, shared:]], 0)
+    value = value * scale + jnp.where(lane == row, prior[...], 0.0)
+    out[...] = eliminate([value], 0)[0]
 
 
 def last_factor(x, prior, scale):
-    shared = x.shape[0]
+    shared = prior.shape[0]
     return pl.pallas_call(
         functools.partial(last_kernel, scale),
         out_shape=jax.ShapeDtypeStruct((shared, shared), F32),

time: 92.9 us -> 90.3 us (0.972)
  Pallas kernels: 88 us -> 85.2 us
    pallas_call x1, Pallas kernels: 14.9 us -> 13.1 us  [total_sum(): pl.pallas_call(functools.partial(total_kernel, axes), out_shape=jax.Shape...]
where the time goes in v1:
time: 90.3 us; the launch traced here: 89.7 us
  Pallas kernels  85.2 us (94%)
  local copies, waits for them, and re-layouts  2.37 us (3%)
  other arithmetic  1.5 us (2%)
    pallas_call x1, Pallas kernels, scatter_sum(): pl.pallas_call(functools.partial(scatter_kernel, n, own), out_shape=jax.S...  25.6 us
    pallas_call x1, Pallas kernels, factor_scenes(): pl.pallas_call(factor_kernel, in_specs=[pl.BlockSpec(memory_space=pltpu.S...  24.2 us
    pallas_call x1, Pallas kernels, merged_partials(): pl.pallas_call(functools.partial(gram_kernel, chunk, scenes), grid_spec=p...  15.4 us
    pallas_call x1, Pallas kernels, total_sum(): pl.pallas_call(functools.partial(total_kernel, axes), out_shape=jax.Shape...  13.1 us
    pallas_call x1, Pallas kernels, last_factor(): pl.pallas_call(functools.partial(last_kernel, scale), out_shape=jax.Shape...  6.86 us

profile of v1, /device:TPU:0, one launch (start us, length us, event | category | flops | bytes accessed | tf_op | source)
XLA Modules:
  0.0 89.7 jit_solution(2293691526619693867)
XLA Ops:
  0.6 0.0 copy-start
  0.7 1.3 %convert_reduce_fusion = (s32[96]{0:T(128)}, pred[16,96]{1,0:T(8,128)(4,1)S(1)}) fusion(s32[16,96]{1,0:T(8,128)} %param.8), kind=kLoop, calls=%fused_computation.4 | loop fusion | flops 4512 | bytes 8064 | tf_op jit(solution)/shard_map/reduce_sum | solution.py:75
  2.0 0.1 multiply_reduce_fusion
  2.2 0.1 copy.14
  2.3 0.7 reshape.25.order
  3.0 15.4 %grams.1.part = f32[16,384,128]{2,1,0:T(8,128)} custom-call(s32[96]{0:T(128)} %counts.1, s32[1536]{0:T(1024)} %reshape.25.order, s32[96]{0:T(128)} %get-tuple-element.6.active, bf16[96,256,256]{2,1,0:T(8,128)(2,1)} %rows_ref.1), custom_call_target="tpu_custom_call" | custom-call | tf_op jit(solution)/shard_map/grams/pallas_call | solution.py:64
  18.4 0.0 copy-start.1
  18.4 25.6 %scatter.1.merged = f32[4,384,128]{2,1,0:T(8,128)} custom-call(f32[16,384,128]{2,1,0:T(8,128)} %grams.1.part), custom_call_target="tpu_custom_call" | custom-call | tf_op jit(solution)/shard_map/scatter/pallas_call | solution.py:142
  44.0 0.0 copy-done
  44.0 0.9 pad.4.sens
  44.9 24.2 %factor.1 = (f32[4,192,256]{2,1,0:T(8,128)}, f32[32,128]{1,0:T(8,128)}) custom-call(f32[4]{0:T(128)} %damping.1, f32[4,384,128]{2,1,0:T(8,128)} %scatter.1.merged, bf16[4,256,256]{2,1,0:T(8,128)(2,1)} %pad.4.sens), custom_call_target="tpu_custom_call" | custom-call | tf_op jit(solution)/shard_map/factor/pallas_call | solution.py:226
  69.1 13.1 %total.1.x = f32[32,128]{1,0:T(8,128)} custom-call(f32[32,128]{1,0:T(8,128)} %get-tuple-element.5.x), custom_call_target="tpu_custom_call" | custom-call | tf_op jit(solution)/shard_map/total/pallas_call | solution.py:282
  82.2 0.0 copy-done.1
  82.2 0.7 copy.15.prior
  82.9 6.9 %last.1 = f32[64,64]{1,0:T(8,128)} custom-call(f32[32,128]{1,0:T(8,128)} %total.1.x, f32[64,1]{1,0:T(8,128)} %copy.15.prior), custom_call_target="tpu_custom_call" | custom-call | tf_op jit(solution)/shard_map/last/pallas_call | solution.py:305
  (5 shorter events, 0.1 us)
Async XLA Ops:
  0.6 43.4 %copy-start = (bf16[16,192,192]{2,1,0:T(8,128)(2,1)S(1)}, bf16[16,192,192]{2,1,0:T(8,128)(2,1)}, u32[]{:S(2)}) copy-start(bf16[16,192,192]{2,1,0:T(8,128)(2,1)} %param.9) | copy-start | bytes 3538948
  18.4 63.8 %copy-start.1 = (f32[64]{0:T(128)S(1)}, f32[64]{0:T(128)}, u32[]{:S(2)}) copy-start(f32[64]{0:T(128)} %param.11) | copy-start | bytes 772
